TPU v7x, 32 devices: a whole 2x2x4 slice. The times are simulated.
32 devices in a mesh: dp: 8 (over z, x), th: 2 (over core), tw: 2 (over y).
Axes of the slice: x: 2, y: 2, z: 4, core: 2. Of those that a mesh axis runs over, the one named last changes fastest.
Arguments:
- tokens: bfloat16 [16, 1536, 768], P('dp', ('th', 'tw')), may hold values from -6 to 6
- segment_ids: int32 [16, 1536], P('dp'), may hold values from 0 to 7, never falling along the last dimension, each value on 1 to 768 neighbouring positions
- norm1_gain: float32 [768], replicated, may hold values from 0.5 to 1.5
- norm1_shift: float32 [768], replicated, may hold values from -3 to 3
- w_qkv: bfloat16 [3, 768, 768], P(None, None, ('th', 'tw')), may hold values from -0.21875 to 0.21875
- b_qv: float32 [2, 768], P(None, ('th', 'tw')), may hold values from -3 to 3
- w_out: bfloat16 [768, 768], P(('th', 'tw')), may hold values from -0.875 to 0.875
- b_out: float32 [768], replicated, may hold values from -3 to 3
- norm2_gain: float32 [768], replicated, may hold values from 0.5 to 1.5
- norm2_shift: float32 [768], replicated, may hold values from -3 to 3
- w_up: bfloat16 [768, 3072], replicated, may hold values from -0.21875 to 0.21875
- b_up: float32 [3072], replicated, may hold values from -3 to 3
- w_down: bfloat16 [3072, 768], replicated, may hold values from -0.109375 to 0.109375
- b_down: float32 [768], replicated, may hold values from -3 to 3
- cotangent: bfloat16 [16, 1536, 768], P('dp', ('th', 'tw')), may hold values from -6 to 6
Outputs:
- block_out: bfloat16 [16, 1536, 768], P('dp', ('th', 'tw'))
- grad_tokens: bfloat16 [16, 1536, 768], P('dp', ('th', 'tw'))
- grad_norm1_gain: float32 [768], replicated
- grad_norm1_shift: float32 [768], replicated
- grad_w_qkv: float32 [3, 768, 768], P(None, None, ('th', 'tw'))
- grad_b_qv: float32 [2, 768], P(None, ('th', 'tw'))
- grad_w_out: float32 [768, 768], P(('th', 'tw'))
- grad_b_out: float32 [768], replicated
- grad_norm2_gain: float32 [768], replicated
- grad_norm2_shift: float32 [768], replicated
- grad_w_up: float32 [768, 3072], replicated
- grad_b_up: float32 [3072], replicated
- grad_w_down: float32 [3072, 768], replicated
- grad_b_down: float32 [768], replicated
Inputs may be any that keep to these rules, and one draw needn't show every extreme that they name: `segment_ids`: within each row the ids never fall, and one image holds 1 to 768 tokens.
All inputs are finite; a program needn't handle non-finite values.
Results may differ from a plain program's by a relative error of at most 0.015.
Values may be sent and summed in bfloat16 or wider, within the bound.
A program may use at most 192 MiB of HBM per device.

v0:
```python
import jax
import jax.numpy as jnp
from jax import lax
from jax.sharding import PartitionSpec as P

HD = 64
EPSILON = 1e-06


def layer_norm(field, norm_gain, norm_shift):
    average = jnp.mean(field, axis=-1, keepdims=True)
    centred = field - average
    spread = jnp.mean(centred * centred, axis=-1, keepdims=True)
    return centred * lax.rsqrt(spread + EPSILON) * norm_gain + norm_shift


def gelu_exact(field):
    return jax.nn.gelu(field, approximate=False)


def masked_scores(query_block, key_rows, row_seg, offset, block_rows):
    score_scale = query_block.shape[-1] ** (-0.5)
    same_image = row_seg[offset : offset + block_rows, None] == row_seg[None, :]
    scores = (
        jnp.einsum("qhe,khe->hqk", query_block, key_rows, preferred_element_type=jnp.float32)
        * score_scale
    )
    return jnp.where(same_image[None], scores, -1000000000.0)


def row_forward(row_items):
    row_qkv, row_seg = row_items
    length = row_qkv.shape[1]
    head_count = row_qkv.shape[2] // HD
    key_rows = row_qkv[1].reshape(length, head_count, HD)
    value_rows = row_qkv[2].reshape(length, head_count, HD)
    block_rows = min(512, length)
    head_outs = []
    log_totals = []
    for offset in range(0, length, block_rows):
        query_block = row_qkv[0, offset : offset + block_rows].reshape(block_rows, head_count, HD)
        scores = masked_scores(query_block, key_rows, row_seg, offset, block_rows)
        row_peak = jnp.max(scores, axis=-1, keepdims=True)
        exponent = jnp.exp(scores - row_peak)
        denominator = jnp.sum(exponent, axis=-1, keepdims=True)
        weights_low = (exponent / denominator).astype(jnp.bfloat16)
        head_out = jnp.einsum(
            "hqk,khe->qhe", weights_low, value_rows, preferred_element_type=jnp.float32
        )
        head_outs.append(head_out.reshape(block_rows, head_count * HD).astype(jnp.bfloat16))
        log_totals.append((row_peak + jnp.log(denominator))[..., 0])
    return (jnp.concatenate(head_outs, 0), jnp.concatenate(log_totals, 1))


def row_backward(row_items):
    row_qkv, row_grad, row_total, row_seg = row_items
    length = row_qkv.shape[1]
    head_count = row_qkv.shape[2] // HD
    score_scale = HD ** (-0.5)
    key_rows = row_qkv[1].reshape(length, head_count, HD)
    value_rows = row_qkv[2].reshape(length, head_count, HD)
    block_rows = min(512, length)
    key_grad = jnp.zeros((length, head_count, HD), jnp.float32)
    value_grad = jnp.zeros((length, head_count, HD), jnp.float32)
    query_grads = []
    for offset in range(0, length, block_rows):
        query_block = row_qkv[0, offset : offset + block_rows].reshape(block_rows, head_count, HD)
        upstream = row_grad[offset : offset + block_rows].reshape(block_rows, head_count, HD)
        scores = masked_scores(query_block, key_rows, row_seg, offset, block_rows)
        probability = jnp.exp(scores - row_total[:, offset : offset + block_rows, None])
        value_grad = value_grad + jnp.einsum(
            "hqk,qhe->khe",
            probability.astype(jnp.bfloat16),
            upstream,
            preferred_element_type=jnp.float32,
        )
        prob_grad = jnp.einsum(
            "qhe,khe->hqk", upstream, value_rows, preferred_element_type=jnp.float32
        )
        row_inner = jnp.sum(probability * prob_grad, axis=-1, keepdims=True)
        score_grad = (probability * (prob_grad - row_inner)).astype(jnp.bfloat16) * score_scale
        query_grad = jnp.einsum(
            "hqk,khe->qhe", score_grad, key_rows, preferred_element_type=jnp.float32
        )
        query_grads.append(query_grad.reshape(block_rows, head_count * HD))
        key_grad = key_grad + jnp.einsum(
            "hqk,qhe->khe", score_grad, query_block, preferred_element_type=jnp.float32
        )
    stacked = jnp.stack(
        [
            jnp.concatenate(query_grads, 0),
            key_grad.reshape(length, head_count * HD),
            value_grad.reshape(length, head_count * HD),
        ]
    )
    return stacked.astype(jnp.bfloat16)


def body(
    tokens,
    segment_ids,
    norm1_gain,
    norm1_shift,
    w_qkv,
    b_qv,
    w_out,
    b_out,
    norm2_gain,
    norm2_shift,
    w_up,
    b_up,
    w_down,
    b_down,
    cotangent,
):
    inputs = tokens.astype(jnp.float32)
    normed_one, norm_one_back = jax.vjp(layer_norm, inputs, norm1_gain, norm1_shift)
    normed_low = normed_one.astype(jnp.bfloat16)
    gathered = lax.all_gather(normed_low, ("th", "tw"), axis=1, tiled=True)
    bias_rows = jnp.stack([b_qv[0], jnp.zeros_like(b_qv[0]), b_qv[1]])
    projected = jnp.einsum("rld,cde->rcle", gathered, w_qkv, preferred_element_type=jnp.float32)
    projected_low = (projected + bias_rows[None, :, None, :]).astype(jnp.bfloat16)
    heads_out, totals = lax.map(row_forward, (projected_low, segment_ids))
    partial_out = jnp.einsum("rle,ed->rld", heads_out, w_out, preferred_element_type=jnp.float32)
    branch = (
        lax.psum_scatter(
            partial_out.astype(jnp.bfloat16), ("th", "tw"), scatter_dimension=1, tiled=True
        ).astype(jnp.float32)
        + b_out
    )
    middle = inputs + branch
    normed_two, norm_two_back = jax.vjp(layer_norm, middle, norm2_gain, norm2_shift)
    second_low = normed_two.astype(jnp.bfloat16)
    hidden_pre = (
        jnp.einsum("rld,df->rlf", second_low, w_up, preferred_element_type=jnp.float32) + b_up
    )
    activated, gelu_back = jax.vjp(gelu_exact, hidden_pre)
    active_low = activated.astype(jnp.bfloat16)
    block_out = middle + (
        jnp.einsum("rlf,fd->rld", active_low, w_down, preferred_element_type=jnp.float32) + b_down
    )
    upstream = cotangent.astype(jnp.float32)
    grad_w_down = jnp.einsum(
        "rlf,rld->fd", active_low, cotangent, preferred_element_type=jnp.float32
    )
    grad_b_down = jnp.sum(upstream, axis=(0, 1))
    grad_active = jnp.einsum("rld,fd->rlf", cotangent, w_down, preferred_element_type=jnp.float32)
    grad_hidden = gelu_back(grad_active)[0].astype(jnp.bfloat16)
    grad_w_up = jnp.einsum(
        "rld,rlf->df", second_low, grad_hidden, preferred_element_type=jnp.float32
    )
    grad_b_up = jnp.sum(grad_hidden.astype(jnp.float32), axis=(0, 1))
    grad_normed_two = jnp.einsum(
        "rlf,df->rld", grad_hidden, w_up, preferred_element_type=jnp.float32
    )
    grad_mid_norm, grad_gain_two, grad_shift_two = norm_two_back(grad_normed_two)
    grad_middle = upstream + grad_mid_norm
    grad_branch = grad_middle.astype(jnp.bfloat16)
    grad_b_out = jnp.sum(grad_branch.astype(jnp.float32), axis=(0, 1))
    grad_whole = lax.all_gather(grad_branch, ("th", "tw"), axis=1, tiled=True)
    grad_heads = jnp.einsum(
        "rld,ed->rle", grad_whole, w_out, preferred_element_type=jnp.float32
    ).astype(jnp.bfloat16)
    grad_w_out = jnp.einsum(
        "rle,rld->ed", heads_out, grad_whole, preferred_element_type=jnp.float32
    )
    grad_qkv = lax.map(row_backward, (projected_low, grad_heads, totals, segment_ids))
    grad_w_qkv = jnp.einsum("rld,rcle->cde", gathered, grad_qkv, preferred_element_type=jnp.float32)
    grad_b_qv = jnp.sum(grad_qkv[:, 0::2].astype(jnp.float32), axis=(0, 2))
    grad_normed = jnp.einsum("rcle,cde->rld", grad_qkv, w_qkv, preferred_element_type=jnp.float32)
    grad_tile = lax.psum_scatter(
        grad_normed.astype(jnp.bfloat16), ("th", "tw"), scatter_dimension=1, tiled=True
    ).astype(jnp.float32)
    grad_inputs, grad_gain_one, grad_shift_one = norm_one_back(grad_tile)
    grad_tokens = (grad_middle + grad_inputs).astype(jnp.bfloat16)
    head_sums = (
        lax.psum(grad_w_qkv.astype(jnp.bfloat16), "dp").astype(jnp.float32),
        lax.psum(grad_b_qv.astype(jnp.bfloat16), "dp").astype(jnp.float32),
        lax.psum(grad_w_out.astype(jnp.bfloat16), "dp").astype(jnp.float32),
    )
    shared = lax.psum(
        (
            grad_gain_one,
            grad_shift_one,
            grad_b_out,
            grad_gain_two,
            grad_shift_two,
            grad_w_up,
            grad_b_up,
            grad_w_down,
            grad_b_down,
        ),
        ("dp", "th", "tw"),
    )
    return (
        block_out.astype(jnp.bfloat16),
        grad_tokens,
        shared[0],
        shared[1],
        head_sums[0],
        head_sums[1],
        head_sums[2],
        shared[2],
        shared[3],
        shared[4],
        shared[5],
        shared[6],
        shared[7],
        shared[8],
    )


def solution(mesh):
    return jax.shard_map(
        body,
        mesh=mesh,
        in_specs=(
            P("dp", ("th", "tw"), None),
            P("dp", None),
            P(),
            P(),
            P(None, None, ("th", "tw")),
            P(None, ("th", "tw")),
            P(("th", "tw"), None),
            P(),
            P(),
            P(),
            P(),
            P(),
            P(),
            P(),
            P("dp", ("th", "tw"), None),
        ),
        out_specs=(
            P("dp", ("th", "tw"), None),
            P("dp", ("th", "tw"), None),
            P(),
            P(),
            P(None, None, ("th", "tw")),
            P(None, ("th", "tw")),
            P(("th", "tw"), None),
            P(),
            P(),
            P(),
            P(),
            P(),
            P(),
            P(),
        ),
        check_vma=False,
    )
```

profile of v0, /device:TPU:0, one launch (start us, length us, event | category | flops | bytes accessed | tf_op | source)
XLA Modules:
  0.0 1006.1 jit_solution(13144696597506998621)
XLA Ops:
  11.7 2.8 fusion.160
  14.8 40.1 %all-gather.3.cloned.1.call-done = bf16[2,1536,768]{2,1,0:T(8,128)(2,1)} async-done(((bf16[2,384,768]{2,1,0:T(8,128)(2,1)}), bf16[2,1536,768]{2,1,0:T(8,128)(2,1)}) %all-gather.3.cloned.1.call-update) | async-done | bytes 4718608 | tf_op jit(solution)/shard_map/all_gather | solution.py:119
  54.9 6.7 fusion.154
  61.6 59.3 %while.22 = (s32[]{:T(128)}, bf16[2,1536,192]{1,2,0:T(8,128)(2,1)S(1)}, f32[2,3,1536]{2,1,0:T(4,128)S(1)}, bf16[2,3,1536,192]{2,3,1,0:T(8,128)(2,1)}, s32[2,1536...) while((s32[]{:T(128)}, bf16[2,1536,192]{1,2,0:T(8,128)(2,1)S(1)}, ...), condition=%wide.region_9.10_spmd, body=%wide.region_2.9_spmd.sunk | while | flops 1901302272 | bytes 107581632 | solution.py:123
  68.4 2.8 fusion.320
  71.2 3.5 fusion.321
  78.7 5.2 fusion.324
  83.9 3.5 fusion.326
  87.4 3.5 fusion.325
  97.6 2.8 fusion.320
  100.4 3.5 fusion.321
  108.0 5.2 fusion.324
  113.1 3.5 fusion.326
  116.7 3.5 fusion.325
  120.9 4.9 convolution_convert_fusion
  125.9 47.9 %reduce-scatter.3.cloned.1.call-done = bf16[2,384,768]{2,1,0:T(8,128)(2,1)} async-done(((bf16[2,1536,768]{2,1,0:T(8,128)(2,1)}), bf16[2,384,768]{2,1,0:T(8,128)(2,1)}) %reduce-scatter.3.cloned.1.call-update) | async-done | bytes 1179664 | tf_op jit(solution)/shard_map/reduce_scatter | solution.py:126
  177.7 9.2 fusion.165
  186.9 23.4 %multiply_convert_fusion.3 = (bf16[2,384,3072]{2,1,0:T(8,128)(2,1)}, f32[2,384,3072]{2,1,0:T(8,128)}) fusion(f32[2,384,3072]{2,1,0:T(8,128)S(1)} %get-tuple-element.164, f32[3072]{0:T(1024)S(1)} %copy-done.45, u8[384,3072]{1,0:T(8,128)(4,1)S(1)} %get-tuple-element.78, u8[384,3072]{1,0:T(8,128)(4,1)S(1)} %get-tuple-element.77), kind=kLoop, calls=%fused_computation.126 | loop fusion | flops 167510016 | bytes 25964544 | tf_op jit(solution)/shard_map/convert_element_type | solution.py:138
  210.2 12.5 %convert_reduce_fusion = (f32[3072]{0:T(1024)}, bf16[2,384,3072]{2,1,0:T(8,128)(2,1)}) fusion(f32[2,384,3072]{2,1,0:T(8,128)} %get-tuple-element.123, bf16[2,384,768]{2,1,0:T(8,128)(2,1)S(1)} %copy-done.15, bf16[3072,768]{1,0:T(8,128)(2,1)} %param.31, f32[2,384,3072]{2,1,0:T(8,128)S(1)} %get-tuple-element.164, f32[3072]{0:T(1024)S(1)} %copy-done.45), kind=kOutput, calls=%fused_computation.124 | convolution fusion | flops 3663983616 | bytes 29515776 | tf_op jit(solution)/shard_map/rld,fd->rlf/dot_general | solution.py:147
  222.8 8.1 fusion.185
  232.9 2.7 convert_reduce_fusion.4
  235.7 37.6 %all-gather.5.cloned.1.call-done = bf16[2,1536,768]{2,1,0:T(8,128)(2,1)} async-done(((bf16[2,384,768]{2,1,0:T(8,128)(2,1)}), bf16[2,1536,768]{2,1,0:T(8,128)(2,1)}) %all-gather.5.cloned.1.call-update) | async-done | bytes 4718608 | tf_op jit(solution)/shard_map/all_gather | solution.py:160
  273.3 5.0 convolution_convert_fusion.1
  278.3 254.2 %while.23 = (s32[]{:T(128)}, bf16[2,3,1536,192]{2,3,1,0:T(8,128)(2,1)}, bf16[2,3,1536,192]{2,3,1,0:T(8,128)(2,1)}, s32[2,1536]{1,0:T(2,128)S(1)}, f32[2,3,1536]{...) while((s32[]{:T(128)}, ...), condition=%wide.region_19.20_spmd, body=%wide.region_15.19_spmd.sunk | while | flops 4682926080 | bytes 364640672 | solution.py:167
  283.2 2.5 subtract_exponential_fusion.9
  286.7 2.6 copy-done.2
  289.3 2.5 subtract_exponential_fusion.11
  294.2 4.3 copy-done.3
  300.4 5.2 fusion.371
  305.6 15.2 %fusion.377 = bf16[3,64,512]{2,1,0:T(8,128)(2,1)} fusion(bf16[1536,3,64]{0,2,1:T(8,128)(2,1)S(1)} %bitcast.312, f32[3,512,1536]{2,1,0:T(8,128)} %copy-done.4, f32[3,512,1536]{2,1,0:T(8,128)} %fusion.371), kind=kOutput, calls=%fused_computation.94.clone.1 | convolution fusion | flops 320965632 | bytes 19660800 | tf_op jit(solution)/shard_map/while/body/eval_jaxpr/hqk,khe->qhe/dot_general | solution.py:82
  320.8 15.3 %fusion.372 = f32[3,64,1536]{2,1,0:T(8,128)} fusion(bf16[512,3,64]{0,2,1:T(8,128)(2,1)} %bitcast.323, f32[3,512,1536]{2,1,0:T(8,128)} %copy-done.4, f32[3,512,1536]{2,1,0:T(8,128)} %fusion.371), kind=kOutput, calls=%fused_computation.63.clone.1 | convolution fusion | flops 320867328 | bytes 20250624 | tf_op jit(solution)/shard_map/while/body/eval_jaxpr/hqk,qhe->khe/dot_general | solution.py:86
  336.1 5.2 fusion.375
  341.3 14.4 %fusion.379 = bf16[3,64,512]{2,1,0:T(8,128)(2,1)S(1)} fusion(bf16[1536,3,64]{0,2,1:T(8,128)(2,1)S(1)} %bitcast.313, f32[3,512,1536]{2,1,0:T(8,128)} %copy-done.3, f32[3,512,1536]{2,1,0:T(8,128)} %fusion.375), kind=kOutput, calls=%fused_computation.92.clone.1 | convolution fusion | flops 320965632 | bytes 19660800 | tf_op jit(solution)/shard_map/while/body/eval_jaxpr/hqk,khe->qhe/dot_general | solution.py:82
  355.6 5.2 fusion.373
  360.8 15.0 %fusion.378 = bf16[3,64,512]{2,1,0:T(8,128)(2,1)} fusion(bf16[1536,3,64]{0,2,1:T(8,128)(2,1)S(1)} %bitcast.314, f32[3,512,1536]{2,1,0:T(8,128)} %copy-done.2, f32[3,512,1536]{2,1,0:T(8,128)} %fusion.373), kind=kOutput, calls=%fused_computation.93.clone.1 | convolution fusion | flops 320965632 | bytes 19660800 | tf_op jit(solution)/shard_map/while/body/eval_jaxpr/hqk,khe->qhe/dot_general | solution.py:82
  375.8 14.1 %fusion.374 = f32[3,64,1536]{2,1,0:T(8,128)} fusion(bf16[512,3,64]{0,2,1:T(8,128)(2,1)S(1)} %bitcast.321, f32[3,512,1536]{2,1,0:T(8,128)} %copy-done.2, f32[3,512,1536]{2,1,0:T(8,128)} %fusion.373), kind=kOutput, calls=%fused_computation.67.clone.1 | convolution fusion | flops 320867328 | bytes 20250624 | tf_op jit(solution)/shard_map/while/body/eval_jaxpr/hqk,qhe->khe/dot_general | solution.py:86
  389.9 14.1 %fusion.376 = bf16[3,64,1536]{2,1,0:T(8,128)(2,1)S(1)} fusion(f32[3,64,1536]{2,1,0:T(8,128)} %fusion.372, f32[3,64,1536]{2,1,0:T(8,128)} %fusion.374, bf16[512,3,64]{0,2,1:T(8,128)(2,1)S(1)} %bitcast.319, f32[3,512,1536]{2,1,0:T(8,128)} %copy-done.3, f32[3,512,1536]{2,1,0:T(8,128)} %fusion.375), kind=kOutput, calls=%fused_computation.79.clone.1 | convolution fusion | flops 321752064 | bytes 22020096 | tf_op jit(solution)/shard_map/while/body/eval_jaxpr/hqk,qhe->khe/dot_general | solution.py:86
  413.5 2.6 copy-done.2
  421.0 4.3 copy-done.3
  427.2 5.2 fusion.371
  432.4 15.2 %fusion.377 = bf16[3,64,512]{2,1,0:T(8,128)(2,1)} fusion(bf16[1536,3,64]{0,2,1:T(8,128)(2,1)S(1)} %bitcast.312, f32[3,512,1536]{2,1,0:T(8,128)} %copy-done.4, f32[3,512,1536]{2,1,0:T(8,128)} %fusion.371), kind=kOutput, calls=%fused_computation.94.clone.1 | convolution fusion | flops 320965632 | bytes 19660800 | tf_op jit(solution)/shard_map/while/body/eval_jaxpr/hqk,khe->qhe/dot_general | solution.py:82
  447.6 15.3 %fusion.372 = f32[3,64,1536]{2,1,0:T(8,128)} fusion(bf16[512,3,64]{0,2,1:T(8,128)(2,1)} %bitcast.323, f32[3,512,1536]{2,1,0:T(8,128)} %copy-done.4, f32[3,512,1536]{2,1,0:T(8,128)} %fusion.371), kind=kOutput, calls=%fused_computation.63.clone.1 | convolution fusion | flops 320867328 | bytes 20250624 | tf_op jit(solution)/shard_map/while/body/eval_jaxpr/hqk,qhe->khe/dot_general | solution.py:86
  462.9 5.2 fusion.375
  468.1 14.4 %fusion.379 = bf16[3,64,512]{2,1,0:T(8,128)(2,1)S(1)} fusion(bf16[1536,3,64]{0,2,1:T(8,128)(2,1)S(1)} %bitcast.313, f32[3,512,1536]{2,1,0:T(8,128)} %copy-done.3, f32[3,512,1536]{2,1,0:T(8,128)} %fusion.375), kind=kOutput, calls=%fused_computation.92.clone.1 | convolution fusion | flops 320965632 | bytes 19660800 | tf_op jit(solution)/shard_map/while/body/eval_jaxpr/hqk,khe->qhe/dot_general | solution.py:82
  482.5 5.2 fusion.373
  487.6 15.0 %fusion.378 = bf16[3,64,512]{2,1,0:T(8,128)(2,1)} fusion(bf16[1536,3,64]{0,2,1:T(8,128)(2,1)S(1)} %bitcast.314, f32[3,512,1536]{2,1,0:T(8,128)} %copy-done.2, f32[3,512,1536]{2,1,0:T(8,128)} %fusion.373), kind=kOutput, calls=%fused_computation.93.clone.1 | convolution fusion | flops 320965632 | bytes 19660800 | tf_op jit(solution)/shard_map/while/body/eval_jaxpr/hqk,khe->qhe/dot_general | solution.py:82
  502.6 14.1 %fusion.374 = f32[3,64,1536]{2,1,0:T(8,128)} fusion(bf16[512,3,64]{0,2,1:T(8,128)(2,1)S(1)} %bitcast.321, f32[3,512,1536]{2,1,0:T(8,128)} %copy-done.2, f32[3,512,1536]{2,1,0:T(8,128)} %fusion.373), kind=kOutput, calls=%fused_computation.67.clone.1 | convolution fusion | flops 320867328 | bytes 20250624 | tf_op jit(solution)/shard_map/while/body/eval_jaxpr/hqk,qhe->khe/dot_general | solution.py:86
  516.8 14.1 %fusion.376 = bf16[3,64,1536]{2,1,0:T(8,128)(2,1)S(1)} fusion(f32[3,64,1536]{2,1,0:T(8,128)} %fusion.372, f32[3,64,1536]{2,1,0:T(8,128)} %fusion.374, bf16[512,3,64]{0,2,1:T(8,128)(2,1)S(1)} %bitcast.319, f32[3,512,1536]{2,1,0:T(8,128)} %copy-done.3, f32[3,512,1536]{2,1,0:T(8,128)} %fusion.375), kind=kOutput, calls=%fused_computation.79.clone.1 | convolution fusion | flops 321752064 | bytes 22020096 | tf_op jit(solution)/shard_map/while/body/eval_jaxpr/hqk,qhe->khe/dot_general | solution.py:86
  532.5 4.6 fusion.177
  537.2 6.2 fusion.174
  543.4 7.7 bitcast_convert_fusion
  551.2 10.5 %convolution_bitcast_fusion = f32[3072,768]{1,0:T(8,128)} fusion(bf16[2,384,3072]{2,1,0:T(8,128)(2,1)} %get-tuple-element.122, bf16[2,384,768]{2,1,0:T(8,128)(2,1)} %param.33), kind=kOutput, calls=%fused_computation.140 | convolution fusion | flops 3623878656 | bytes 15335424 | tf_op jit(solution)/shard_map/rlf,rld->fd/dot_general | solution.py:143
  561.7 9.2 convolution_bitcast_fusion.1
  571.7 8.8 add_convert_fusion.3
  580.9 21.5 %psum.87 = bf16[2,192]{1,0:T(2,128)(2,1)S(1)} all-reduce(bf16[2,192]{1,0:T(2,128)(2,1)S(1)} %slice_reduce_fusion), channel_id=1, replica_groups=mesh['dp'=8,'th'=2,'tw'=2] {'dp'}, use_global_device_ids=true, to_apply=%region_29.30 | all-reduce | flops 384 | bytes 1536 | tf_op jit(solution)/shard_map/psum | solution.py:178
  603.0 20.8 %all-reduce.8.cloned.1.call-done = (bf16[3,768,192]{1,2,0:T(8,128)(2,1)}, bf16[192,768]{1,0:T(8,128)(2,1)}) async-done(((bf16[3,768,192]{1,2,0:T(8,128)(2,1)}, bf16[192,768]{1,0:T(8,128)(2,1)}), (bf16[3,768,192]{1,2,0:T(8,128)(2,1)}, bf16[192,768]{1,0:T(8,128)(2,1)})) %all-reduce.8.cloned.1.call-update) | async-done | bytes 1179664 | tf_op jit(solution)/shard_map/psum | solution.py:177
  625.6 2.5 convert_element_type.154
  628.1 45.2 %reduce-scatter.5.cloned.1.call-done = bf16[2,384,768]{2,1,0:T(8,128)(2,1)} async-done(((bf16[2,1536,768]{2,1,0:T(8,128)(2,1)}), bf16[2,384,768]{2,1,0:T(8,128)(2,1)}) %reduce-scatter.5.cloned.1.call-update) | async-done | bytes 1179664 | tf_op jit(solution)/shard_map/reduce_scatter | solution.py:171
  675.6 2.7 fusion.163
  678.4 3.0 convert_reduce_fusion.3
  681.4 42.5 %all-reduce = (f32[768]{0:T(1024)}, f32[768]{0:T(1024)}, f32[768]{0:T(1024)}, f32[768]{0:T(1024)}, f32[768]{0:T(1024)}, /*index=5*/f32[3072]{0:T(1024)}, f32[768]{0:T(1024)}) all-reduce(f32[768]{0:T(1024)S(1)} %get-tuple-element.81, f32[768]{0:T(1024)S(1)} %get-tuple-element.85, ...), channel_id=1, replica_groups=mesh['dp'=8,'th'=2,'tw'=2] {'dp','th','tw'}, use_global_device_ids=true, to_apply=%region_24.25 | all-reduce | flops 7680 | bytes 61440 | tf_op jit(solution)/shard_map/psum | solution.py:181
  724.0 262.5 %all-reduce.6.cloned.1.call-done = (f32[768,3072]{1,0:T(8,128)}, f32[3072,768]{1,0:T(8,128)}) async-done(((f32[768,3072]{1,0:T(8,128)}, f32[3072,768]{1,0:T(8,128)}), (f32[768,3072]{1,0:T(8,128)}, f32[3072,768]{1,0:T(8,128)})) %all-reduce.6.cloned.1.call-update) | async-done | bytes 18874384 | tf_op jit(solution)/shard_map/psum | solution.py:181
  986.5 8.8 copy.59
  995.2 3.7 copy.60
  (212 shorter events, 65.0 us)
Async XLA Ops:
  7.2 47.7 %copy-start = (bf16[3,768,192]{1,2,0:T(8,128)(2,1)S(1)}, bf16[3,768,192]{1,2,0:T(8,128)(2,1)}, u32[]{:S(2)}) copy-start(bf16[3,768,192]{1,2,0:T(8,128)(2,1)} %param.23) | copy-start | bytes 2654212
  7.2 7.5 copy-start.48
  7.2 47.7 %all-gather.3.cloned.1.call-start = ((), (), s32[]{:S(2)}) async-start(), calls=%async_computation.2 | async-start | bytes 5898240 | tf_op jit(solution)/shard_map/all_gather | solution.py:119
  8.8 2.3 copy-start.32
  14.6 159.3 %reduce-scatter.3.cloned.1.call-start = ((), (), s32[]{:S(2)}) async-start(), calls=%async_computation.3 | async-start | bytes 5898240 | tf_op jit(solution)/shard_map/reduce_scatter | solution.py:126
  14.8 46.8 %copy-start.20 = (s32[2,1536]{1,0:T(2,128)S(1)}, s32[2,1536]{1,0:T(2,128)}, u32[]{:S(2)}) copy-start(s32[2,1536]{1,0:T(2,128)} %param.20) | copy-start | bytes 36868
  120.8 5.0 copy-start.17
  120.9 53.0 %copy-start.5 = (bf16[2,384,768]{2,1,0:T(8,128)(2,1)S(1)}, bf16[2,384,768]{2,1,0:T(8,128)(2,1)}, u32[]{:S(2)}) copy-start(bf16[2,384,768]{2,1,0:T(8,128)(2,1)} %param.19) | copy-start | bytes 3538948
  120.9 53.0 %copy-start.21 = (f32[768]{0:T(1024)S(1)}, f32[768]{0:T(1024)}, u32[]{:S(2)}) copy-start(f32[768]{0:T(1024)} %param.26) | copy-start | bytes 9220
  125.8 51.8 %copy-start.25 = (f32[768]{0:T(1024)S(1)}, f32[768]{0:T(1024)}, u32[]{:S(2)}) copy-start(f32[768]{0:T(1024)} %param.27) | copy-start | bytes 9220
  125.8 51.8 %copy-start.30 = (f32[768]{0:T(1024)S(1)}, f32[768]{0:T(1024)}, u32[]{:S(2)}) copy-start(f32[768]{0:T(1024)} %param.28) | copy-start | bytes 9220
  125.8 51.8 %copy-start.45 = (f32[3072]{0:T(1024)S(1)}, f32[3072]{0:T(1024)}, u32[]{:S(2)}) copy-start(f32[3072]{0:T(1024)} %param.30) | copy-start | bytes 36868
  125.8 147.5 %all-gather.5.cloned.1.call-start = ((), (), s32[]{:S(2)}) async-start(), calls=%async_computation.4 | async-start | bytes 5898240 | tf_op jit(solution)/shard_map/all_gather | solution.py:160
  173.8 3.8 copy-start.7
  175.7 57.2 %copy-start.23 = (f32[2,384]{1,0:T(2,128)}, f32[2,384]{1,0:T(2,128)S(1)}, u32[]{:S(2)}) copy-start(f32[2,384]{1,0:T(2,128)S(1)} %broadcast_multiply_fusion) | copy-start | bytes 9220
  177.7 55.3 %copy-start.27 = (f32[2,384]{1,0:T(2,128)}, f32[2,384]{1,0:T(2,128)S(1)}, u32[]{:S(2)}) copy-start(f32[2,384]{1,0:T(2,128)S(1)} %fusion.183) | copy-start | bytes 9220
  186.8 23.4 %copy-start.15 = (bf16[2,384,768]{2,1,0:T(8,128)(2,1)S(1)}, bf16[2,384,768]{2,1,0:T(8,128)(2,1)}, u32[]{:S(2)}) copy-start(bf16[2,384,768]{2,1,0:T(8,128)(2,1)} %param.33) | copy-start | bytes 3538948
  230.9 4.8 copy-start.9
  230.9 4.8 copy-start.35
  232.9 40.4 %copy-start.29 = (bf16[192,768]{1,0:T(8,128)(2,1)S(1)}, bf16[192,768]{1,0:T(8,128)(2,1)}, u32[]{:S(2)}) copy-start(bf16[192,768]{1,0:T(8,128)(2,1)} %param.25) | copy-start | bytes 884740
  232.9 45.4 %copy-start.39 = (f32[2,384]{1,0:T(2,128)}, f32[2,384]{1,0:T(2,128)S(1)}, u32[]{:S(2)}) copy-start(f32[2,384]{1,0:T(2,128)S(1)} %negate_multiply_fusion.2) | copy-start | bytes 9220
  235.7 388.1 %all-reduce.8.cloned.1.call-start = ((), (), s32[]{:S(2)}) async-start(), calls=%async_computation.7 | async-start | bytes 2359296 | tf_op jit(solution)/shard_map/psum | solution.py:177
  278.7 2.8 copy-start.1
  281.7 4.9 copy-start.12
  285.6 3.6 copy-start.2
  291.7 7.7 copy-start.4
  294.2 4.3 copy-start.3
  389.9 14.2 %copy-start.13 = (bf16[3,64,512]{2,1,0:T(8,128)(2,1)S(1)}, bf16[3,64,512]{2,1,0:T(8,128)(2,1)}, u32[]{:S(2)}) copy-start(bf16[3,64,512]{2,1,0:T(8,128)(2,1)} %fusion.377) | copy-start | bytes 589828 | tf_op jit(solution)/shard_map/while
  389.9 14.2 %copy-start.14 = (bf16[3,64,512]{2,1,0:T(8,128)(2,1)S(1)}, bf16[3,64,512]{2,1,0:T(8,128)(2,1)}, u32[]{:S(2)}) copy-start(bf16[3,64,512]{2,1,0:T(8,128)(2,1)} %fusion.378) | copy-start | bytes 589828 | tf_op jit(solution)/shard_map/while
  405.6 2.8 copy-start.1
  408.6 4.9 copy-start.12
  412.5 3.6 copy-start.2
  418.6 7.7 copy-start.4
  421.0 4.3 copy-start.3
  516.7 14.2 %copy-start.13 = (bf16[3,64,512]{2,1,0:T(8,128)(2,1)S(1)}, bf16[3,64,512]{2,1,0:T(8,128)(2,1)}, u32[]{:S(2)}) copy-start(bf16[3,64,512]{2,1,0:T(8,128)(2,1)} %fusion.377) | copy-start | bytes 589828 | tf_op jit(solution)/shard_map/while
  516.8 14.2 %copy-start.14 = (bf16[3,64,512]{2,1,0:T(8,128)(2,1)S(1)}, bf16[3,64,512]{2,1,0:T(8,128)(2,1)}, u32[]{:S(2)}) copy-start(bf16[3,64,512]{2,1,0:T(8,128)(2,1)} %fusion.378) | copy-start | bytes 589828 | tf_op jit(solution)/shard_map/while
  532.5 4.7 copy-start.18
  543.3 130.0 %reduce-scatter.5.cloned.1.call-start = ((), (), s32[]{:S(2)}) async-start(), calls=%async_computation.5 | async-start | bytes 5898240 | tf_op jit(solution)/shard_map/reduce_scatter | solution.py:171
  551.1 435.4 %all-reduce.6.cloned.1.call-start = ((), (), s32[]{:S(2)}) async-start(), calls=%async_computation.6 | async-start | bytes 37748736 | tf_op jit(solution)/shard_map/psum | solution.py:181
  551.1 10.6 %copy-start.6 = (bf16[2,384,768]{2,1,0:T(8,128)(2,1)S(1)}, bf16[2,384,768]{2,1,0:T(8,128)(2,1)}, u32[]{:S(2)}) copy-start(bf16[2,384,768]{2,1,0:T(8,128)(2,1)} %param.19) | copy-start | bytes 3538948
  551.1 10.6 %copy-start.8 = (bf16[2,384,768]{2,1,0:T(8,128)(2,1)S(1)}, bf16[2,384,768]{2,1,0:T(8,128)(2,1)}, u32[]{:S(2)}) copy-start(bf16[2,384,768]{2,1,0:T(8,128)(2,1)} %reduce-scatter.3.cloned.1.call-done) | copy-start | bytes 3538948
  551.2 10.5 %copy-start.22 = (f32[768]{0:T(1024)S(1)}, f32[768]{0:T(1024)}, u32[]{:S(2)}) copy-start(f32[768]{0:T(1024)} %param.26) | copy-start | bytes 9220
  551.2 10.5 %copy-start.24 = (f32[2,384]{1,0:T(2,128)S(1)}, f32[2,384]{1,0:T(2,128)}, u32[]{:S(2)}) copy-start(f32[2,384]{1,0:T(2,128)} %copy-done.23) | copy-start | bytes 9220
  551.2 10.5 %copy-start.26 = (f32[768]{0:T(1024)S(1)}, f32[768]{0:T(1024)}, u32[]{:S(2)}) copy-start(f32[768]{0:T(1024)} %param.27) | copy-start | bytes 9220
  551.2 10.5 %copy-start.28 = (f32[2,384]{1,0:T(2,128)S(1)}, f32[2,384]{1,0:T(2,128)}, u32[]{:S(2)}) copy-start(f32[2,384]{1,0:T(2,128)} %copy-done.27) | copy-start | bytes 9220
  551.2 10.5 %copy-start.31 = (f32[768]{0:T(1024)S(1)}, f32[768]{0:T(1024)}, u32[]{:S(2)}) copy-start(f32[768]{0:T(1024)} %param.28) | copy-start | bytes 9220
  571.0 0.7 copy-start.49
  571.7 8.8 copy-start.19
  580.5 92.9 %copy-start.33 = (f32[2,384]{1,0:T(2,128)S(1)}, f32[2,384]{1,0:T(2,128)}, u32[]{:S(2)}) copy-start(f32[2,384]{1,0:T(2,128)} %copy-done.32) | copy-start | bytes 9220
  580.5 92.9 %copy-start.34 = (f32[768]{0:T(1024)S(1)}, f32[768]{0:T(1024)}, u32[]{:S(2)}) copy-start(f32[768]{0:T(1024)} %param.21) | copy-start | bytes 9220
  580.5 95.1 %copy-start.42 = (f32[2,384]{1,0:T(2,128)S(1)}, f32[2,384]{1,0:T(2,128)}, u32[]{:S(2)}) copy-start(f32[2,384]{1,0:T(2,128)} %copy-done.41) | copy-start | bytes 9220
  580.5 95.1 %copy-start.38 = (f32[2,384]{1,0:T(2,128)S(1)}, f32[2,384]{1,0:T(2,128)}, u32[]{:S(2)}) copy-start(f32[2,384]{1,0:T(2,128)} %copy-done.37) | copy-start | bytes 9220
  580.9 97.5 %copy-start.36 = (f32[2,384]{1,0:T(2,128)S(1)}, f32[2,384]{1,0:T(2,128)}, u32[]{:S(2)}) copy-start(f32[2,384]{1,0:T(2,128)} %copy-done.35) | copy-start | bytes 9220
  580.9 97.5 %copy-start.40 = (f32[2,384]{1,0:T(2,128)S(1)}, f32[2,384]{1,0:T(2,128)}, u32[]{:S(2)}) copy-start(f32[2,384]{1,0:T(2,128)} %copy-done.39) | copy-start | bytes 9220
  673.3 5.1 copy-start.10
  673.3 5.1 copy-start.11
  673.3 5.1 copy-start.16
  678.3 3.1 copy-start.43
  678.3 3.1 copy-start.44
  678.3 3.1 copy-start.46
  678.4 3.1 copy-start.47
  986.5 8.8 slice-start
  986.5 8.8 slice-start.1
  986.5 8.8 slice-start.2
  (2 other events, 1.2 us)
Sparse Core Ops, SparseCore 0:
  14.7 40.1 all-gather.2
  126.0 47.8 reduce-scatter.2
  235.8 37.4 all-gather.4
  543.5 80.2 all-reduce.7
  626.2 47.1 reduce-scatter.4
  681.3 305.1 all-reduce.5
where the time goes:
time: 1010 us
  waiting for transfers between devices  454 us (45%)
  matrix products  354 us (35%)
  other arithmetic  75.9 us (8%)
  blocking collectives  64 us (6%)
  local copies, waits for them, and re-layouts  40.5 us (4%)
  between operations  14.8 us (1%)
    psum x1, waiting for transfers between devices, body(): lax.psum((grad_gain_one, grad_shift_one, grad_b_out, grad_gain_two, grad_...  263 us
    dot_general x6, matrix products, row_backward(): jnp.einsum('hqk,khe->qhe', score_grad, key_rows, preferred_element_type=j...  89.1 us
    dot_general x6, matrix products, row_backward(): jnp.einsum('hqk,qhe->khe', score_grad, query_block, preferred_element_typ...  87.3 us
    reduce_scatter x1, waiting for transfers between devices, body(): lax.psum_scatter(partial_out.astype(jnp.bfloat16), ('th', 'tw'), scatter_...  47.9 us
    reduce_scatter x1, waiting for transfers between devices, body(): lax.psum_scatter(grad_normed.astype(jnp.bfloat16), ('th', 'tw'), scatter_...  45.2 us
    psum x1, blocking collectives, body(): lax.psum((grad_gain_one, grad_shift_one, grad_b_out, grad_gain_two, grad_...  42.5 us
    all_gather x1, waiting for transfers between devices, body(): gathered = lax.all_gather(normed_low, ('th', 'tw'), axis=1, tiled=True)  40.1 us
    all_gather x1, waiting for transfers between devices, body(): grad_whole = lax.all_gather(grad_branch, ('th', 'tw'), axis=1, tiled=True)  37.6 us
  transfers between devices with their start and end apart: 6, of which 6 were waited for; matrix products, arithmetic and copies ran while one was open for 5% of the time, Pallas kernels for 0%

commit v1 on v0

--- a/solution.py
+++ b/solution.py
@@ -178,20 +178,19 @@
         lax.psum(grad_b_qv.astype(jnp.bfloat16), "dp").astype(jnp.float32),
         lax.psum(grad_w_out.astype(jnp.bfloat16), "dp").astype(jnp.float32),
     )
-    shared = lax.psum(
-        (
-            grad_gain_one,
-            grad_shift_one,
-            grad_b_out,
-            grad_gain_two,
-            grad_shift_two,
-            grad_w_up,
-            grad_b_up,
-            grad_w_down,
-            grad_b_down,
-        ),
-        ("dp", "th", "tw"),
-    )
+    shared = (
+        grad_gain_one,
+        grad_shift_one,
+        grad_b_out,
+        grad_gain_two,
+        grad_shift_two,
+        grad_w_up,
+        grad_b_up,
+        grad_w_down,
+        grad_b_down,
+    )
+    for over in (("th", "tw"), "dp"):
+        shared = lax.psum(shared, over)
     return (
         block_out.astype(jnp.bfloat16),
         grad_tokens,

time: 1010 us -> 1330 us (1.32)
  waiting for transfers between devices: 454 us -> 749 us
    psum x1 -> x2, waiting for transfers between devices: 263 us -> 547 us  [body(): shared = lax.psum(shared, over)]
    psum x1, waiting for transfers between devices: 20.8 us -> 51.6 us  [body(): lax.psum(grad_w_qkv.astype(jnp.bfloat16), 'dp').astype(jnp.float32)]
    all_gather x1, waiting for transfers between devices: 37.6 us -> 17.3 us  [body(): grad_whole = lax.all_gather(grad_branch, ('th', 'tw'), axis=1, tiled=True)]
    psum x1 -> x2, blocking collectives: 42.5 us -> 54 us  [body(): shared = lax.psum(shared, over)]
  transfers between devices with their start and end apart: 6 -> 7, of which waited for: 6 -> 7; matrix products, arithmetic and copies ran while one was open for 5% -> 23% of each run, Pallas kernels for 0% -> 0%
where the time goes in v1:
time: 1330 us
  waiting for transfers between devices  749 us (56%)
  matrix products  359 us (27%)
  other arithmetic  75.9 us (6%)
  blocking collectives  75.6 us (6%)
  local copies, waits for them, and re-layouts  41.5 us (3%)
  between operations  14.8 us (1%)
    psum x2, waiting for transfers between devices, body(): shared = lax.psum(shared, over)  547 us
    dot_general x6, matrix products, row_backward(): jnp.einsum('hqk,khe->qhe', score_grad, key_rows, preferred_element_type=j...  91.6 us
    dot_general x6, matrix products, row_backward(): jnp.einsum('hqk,qhe->khe', score_grad, query_block, preferred_element_typ...  90 us
    psum x2, blocking collectives, body(): shared = lax.psum(shared, over)  54 us
    psum x1, waiting for transfers between devices, body(): lax.psum(grad_w_qkv.astype(jnp.bfloat16), 'dp').astype(jnp.float32)  51.6 us
    reduce_scatter x1, waiting for transfers between devices, body(): lax.psum_scatter(partial_out.astype(jnp.bfloat16), ('th', 'tw'), scatter_...  47.9 us
    reduce_scatter x1, waiting for transfers between devices, body(): lax.psum_scatter(grad_normed.astype(jnp.bfloat16), ('th', 'tw'), scatter_...  45.4 us
    all_gather x1, waiting for transfers between devices, body(): gathered = lax.all_gather(normed_low, ('th', 'tw'), axis=1, tiled=True)  40.1 us
  transfers between devices with their start and end apart: 7, of which 7 were waited for; matrix products, arithmetic and copies ran while one was open for 23% of the time, Pallas kernels for 0%

profile of v1, /device:TPU:0, one launch (start us, length us, event | category | flops | bytes accessed | tf_op | source)
XLA Modules:
  0.0 1326.9 jit_solution(14180979223463587359)
XLA Ops:
  11.7 2.8 fusion.160
  14.8 40.1 %all-gather.3.cloned.1.call-done = bf16[2,1536,768]{2,1,0:T(8,128)(2,1)} async-done(((bf16[2,384,768]{2,1,0:T(8,128)(2,1)}), bf16[2,1536,768]{2,1,0:T(8,128)(2,1)}) %all-gather.3.cloned.1.call-update) | async-done | bytes 4718608 | tf_op jit(solution)/shard_map/all_gather | solution.py:119
  54.9 6.7 fusion.154
  61.6 59.1 %while.22 = (s32[]{:T(128)}, bf16[2,1536,192]{1,2,0:T(8,128)(2,1)S(1)}, f32[2,3,1536]{2,1,0:T(4,128)S(1)}, bf16[2,3,1536,192]{2,3,1,0:T(8,128)(2,1)}, s32[2,1536...) while((s32[]{:T(128)}, bf16[2,1536,192]{1,2,0:T(8,128)(2,1)S(1)}, ...), condition=%wide.region_9.10_spmd, body=%wide.region_2.9_spmd.sunk | while | flops 1901302272 | bytes 107581632 | solution.py:123
  68.6 2.8 fusion.320
  71.4 3.5 fusion.321
  78.9 5.2 fusion.324
  84.1 3.5 fusion.326
  87.6 3.5 fusion.325
  97.8 2.8 fusion.320
  100.6 3.5 fusion.321
  108.2 5.2 fusion.324
  113.3 3.5 fusion.326
  116.9 3.5 fusion.325
  120.7 4.9 convolution_convert_fusion
  125.8 47.9 %reduce-scatter.3.cloned.1.call-done = bf16[2,384,768]{2,1,0:T(8,128)(2,1)} async-done(((bf16[2,1536,768]{2,1,0:T(8,128)(2,1)}), bf16[2,384,768]{2,1,0:T(8,128)(2,1)}) %reduce-scatter.3.cloned.1.call-update) | async-done | bytes 1179664 | tf_op jit(solution)/shard_map/reduce_scatter | solution.py:126
  177.5 9.2 fusion.165
  186.7 23.4 %multiply_convert_fusion.3 = (bf16[2,384,3072]{2,1,0:T(8,128)(2,1)}, f32[2,384,3072]{2,1,0:T(8,128)}) fusion(f32[2,384,3072]{2,1,0:T(8,128)S(1)} %get-tuple-element.173, f32[3072]{0:T(1024)S(1)} %copy-done.44, u8[384,3072]{1,0:T(8,128)(4,1)S(1)} %get-tuple-element.78, u8[384,3072]{1,0:T(8,128)(4,1)S(1)} %get-tuple-element.77), kind=kLoop, calls=%fused_computation.126 | loop fusion | flops 167510016 | bytes 25964544 | tf_op jit(solution)/shard_map/convert_element_type | solution.py:138
  210.1 12.5 convert_reduce_fusion
  222.6 8.1 fusion.185
  232.7 2.7 convert_reduce_fusion.4
  236.0 10.8 convolution_bitcast_fusion
  246.7 9.0 convolution_bitcast_fusion.1
  255.8 17.3 %all-gather.5.cloned.1.call-done = bf16[2,1536,768]{2,1,0:T(8,128)(2,1)} async-done(((bf16[2,384,768]{2,1,0:T(8,128)(2,1)}), bf16[2,1536,768]{2,1,0:T(8,128)(2,1)}) %all-gather.5.cloned.1.call-update) | async-done | bytes 4718608 | tf_op jit(solution)/shard_map/all_gather | solution.py:160
  273.1 5.0 convolution_convert_fusion.1
  278.1 267.2 %while.23 = (s32[]{:T(128)}, bf16[2,3,1536,192]{2,3,1,0:T(8,128)(2,1)}, bf16[2,3,1536,192]{2,3,1,0:T(8,128)(2,1)}, s32[2,1536]{1,0:T(2,128)S(1)}, f32[2,3,1536]{...) while((s32[]{:T(128)}, ...), condition=%wide.region_19.20_spmd, body=%wide.region_15.19_spmd.sunk | while | flops 4682926080 | bytes 364640672 | solution.py:167
  286.2 2.7 copy-done.2
  293.8 4.2 copy-done.3
  299.9 4.9 fusion.371
  304.8 15.1 %fusion.377 = bf16[3,64,512]{2,1,0:T(8,128)(2,1)} fusion(bf16[1536,3,64]{0,2,1:T(8,128)(2,1)S(1)} %bitcast.312, f32[3,512,1536]{2,1,0:T(8,128)} %copy-done.4, f32[3,512,1536]{2,1,0:T(8,128)} %fusion.371), kind=kOutput, calls=%fused_computation.94.clone.1 | convolution fusion | flops 320965632 | bytes 19660800 | tf_op jit(solution)/shard_map/while/body/eval_jaxpr/hqk,khe->qhe/dot_general | solution.py:82
  320.0 16.2 %fusion.372 = f32[3,64,1536]{2,1,0:T(8,128)} fusion(bf16[512,3,64]{0,2,1:T(8,128)(2,1)} %bitcast.323, f32[3,512,1536]{2,1,0:T(8,128)} %copy-done.4, f32[3,512,1536]{2,1,0:T(8,128)} %fusion.371), kind=kOutput, calls=%fused_computation.63.clone.1 | convolution fusion | flops 320867328 | bytes 20250624 | tf_op jit(solution)/shard_map/while/body/eval_jaxpr/hqk,qhe->khe/dot_general | solution.py:86
  336.1 5.0 fusion.375
  341.2 14.5 %fusion.379 = bf16[3,64,512]{2,1,0:T(8,128)(2,1)S(1)} fusion(bf16[1536,3,64]{0,2,1:T(8,128)(2,1)S(1)} %bitcast.313, f32[3,512,1536]{2,1,0:T(8,128)} %copy-done.3, f32[3,512,1536]{2,1,0:T(8,128)} %fusion.375), kind=kOutput, calls=%fused_computation.92.clone.1 | convolution fusion | flops 320965632 | bytes 19660800 | tf_op jit(solution)/shard_map/while/body/eval_jaxpr/hqk,khe->qhe/dot_general | solution.py:82
  355.6 4.9 fusion.373
  360.6 15.5 %fusion.378 = bf16[3,64,512]{2,1,0:T(8,128)(2,1)} fusion(bf16[1536,3,64]{0,2,1:T(8,128)(2,1)S(1)} %bitcast.314, f32[3,512,1536]{2,1,0:T(8,128)} %copy-done.2, f32[3,512,1536]{2,1,0:T(8,128)} %fusion.373), kind=kOutput, calls=%fused_computation.93.clone.1 | convolution fusion | flops 320965632 | bytes 19660800 | tf_op jit(solution)/shard_map/while/body/eval_jaxpr/hqk,khe->qhe/dot_general | solution.py:82
  376.1 15.4 %fusion.374 = f32[3,64,1536]{2,1,0:T(8,128)} fusion(bf16[512,3,64]{0,2,1:T(8,128)(2,1)S(1)} %bitcast.321, f32[3,512,1536]{2,1,0:T(8,128)} %copy-done.2, f32[3,512,1536]{2,1,0:T(8,128)} %fusion.373), kind=kOutput, calls=%fused_computation.67.clone.1 | convolution fusion | flops 320867328 | bytes 20250624 | tf_op jit(solution)/shard_map/while/body/eval_jaxpr/hqk,qhe->khe/dot_general | solution.py:86
  391.5 14.2 %fusion.376 = bf16[3,64,1536]{2,1,0:T(8,128)(2,1)S(1)} fusion(f32[3,64,1536]{2,1,0:T(8,128)} %fusion.372, f32[3,64,1536]{2,1,0:T(8,128)} %fusion.374, bf16[512,3,64]{0,2,1:T(8,128)(2,1)S(1)} %bitcast.319, f32[3,512,1536]{2,1,0:T(8,128)} %copy-done.3, f32[3,512,1536]{2,1,0:T(8,128)} %fusion.375), kind=kOutput, calls=%fused_computation.79.clone.1 | convolution fusion | flops 321752064 | bytes 22020096 | tf_op jit(solution)/shard_map/while/body/eval_jaxpr/hqk,qhe->khe/dot_general | solution.py:86
  415.1 2.7 copy-done.2
  422.8 4.3 copy-done.3
  428.9 4.9 fusion.371
  433.9 16.3 %fusion.377 = bf16[3,64,512]{2,1,0:T(8,128)(2,1)} fusion(bf16[1536,3,64]{0,2,1:T(8,128)(2,1)S(1)} %bitcast.312, f32[3,512,1536]{2,1,0:T(8,128)} %copy-done.4, f32[3,512,1536]{2,1,0:T(8,128)} %fusion.371), kind=kOutput, calls=%fused_computation.94.clone.1 | convolution fusion | flops 320965632 | bytes 19660800 | tf_op jit(solution)/shard_map/while/body/eval_jaxpr/hqk,khe->qhe/dot_general | solution.py:82
  450.2 15.4 %fusion.372 = f32[3,64,1536]{2,1,0:T(8,128)} fusion(bf16[512,3,64]{0,2,1:T(8,128)(2,1)} %bitcast.323, f32[3,512,1536]{2,1,0:T(8,128)} %copy-done.4, f32[3,512,1536]{2,1,0:T(8,128)} %fusion.371), kind=kOutput, calls=%fused_computation.63.clone.1 | convolution fusion | flops 320867328 | bytes 20250624 | tf_op jit(solution)/shard_map/while/body/eval_jaxpr/hqk,qhe->khe/dot_general | solution.py:86
  465.6 5.0 fusion.375
  470.6 14.5 %fusion.379 = bf16[3,64,512]{2,1,0:T(8,128)(2,1)S(1)} fusion(bf16[1536,3,64]{0,2,1:T(8,128)(2,1)S(1)} %bitcast.313, f32[3,512,1536]{2,1,0:T(8,128)} %copy-done.3, f32[3,512,1536]{2,1,0:T(8,128)} %fusion.375), kind=kOutput, calls=%fused_computation.92.clone.1 | convolution fusion | flops 320965632 | bytes 19660800 | tf_op jit(solution)/shard_map/while/body/eval_jaxpr/hqk,khe->qhe/dot_general | solution.py:82
  485.1 5.0 fusion.373
  490.1 15.7 %fusion.378 = bf16[3,64,512]{2,1,0:T(8,128)(2,1)} fusion(bf16[1536,3,64]{0,2,1:T(8,128)(2,1)S(1)} %bitcast.314, f32[3,512,1536]{2,1,0:T(8,128)} %copy-done.2, f32[3,512,1536]{2,1,0:T(8,128)} %fusion.373), kind=kOutput, calls=%fused_computation.93.clone.1 | convolution fusion | flops 320965632 | bytes 19660800 | tf_op jit(solution)/shard_map/while/body/eval_jaxpr/hqk,khe->qhe/dot_general | solution.py:82
  505.8 14.6 %fusion.374 = f32[3,64,1536]{2,1,0:T(8,128)} fusion(bf16[512,3,64]{0,2,1:T(8,128)(2,1)S(1)} %bitcast.321, f32[3,512,1536]{2,1,0:T(8,128)} %copy-done.2, f32[3,512,1536]{2,1,0:T(8,128)} %fusion.373), kind=kOutput, calls=%fused_computation.67.clone.1 | convolution fusion | flops 320867328 | bytes 20250624 | tf_op jit(solution)/shard_map/while/body/eval_jaxpr/hqk,qhe->khe/dot_general | solution.py:86
  520.4 14.3 %fusion.376 = bf16[3,64,1536]{2,1,0:T(8,128)(2,1)S(1)} fusion(f32[3,64,1536]{2,1,0:T(8,128)} %fusion.372, f32[3,64,1536]{2,1,0:T(8,128)} %fusion.374, bf16[512,3,64]{0,2,1:T(8,128)(2,1)S(1)} %bitcast.319, f32[3,512,1536]{2,1,0:T(8,128)} %copy-done.3, f32[3,512,1536]{2,1,0:T(8,128)} %fusion.375), kind=kOutput, calls=%fused_computation.79.clone.1 | convolution fusion | flops 321752064 | bytes 22020096 | tf_op jit(solution)/shard_map/while/body/eval_jaxpr/hqk,qhe->khe/dot_general | solution.py:86
  545.3 4.7 fusion.177
  550.0 6.2 fusion.174
  556.3 7.7 bitcast_convert_fusion
  564.1 34.6 %all-reduce.11.cloned.1.call-done = (f32[768,3072]{1,0:T(8,128)}, f32[3072,768]{1,0:T(8,128)}) async-done(((f32[768,3072]{1,0:T(8,128)}, f32[3072,768]{1,0:T(8,128)}), (f32[768,3072]{1,0:T(8,128)}, f32[3072,768]{1,0:T(8,128)})) %all-reduce.11.cloned.1.call-update) | async-done | bytes 18874384 | tf_op jit(solution)/shard_map/psum | solution.py:193
  600.3 8.8 add_convert_fusion.3
  609.6 21.7 %psum.152 = bf16[2,192]{1,0:T(2,128)(2,1)S(1)} all-reduce(bf16[2,192]{1,0:T(2,128)(2,1)S(1)} %slice_reduce_fusion), channel_id=1, replica_groups=mesh['dp'=8,'th'=2,'tw'=2] {'dp'}, use_global_device_ids=true, to_apply=%region_31.32 | all-reduce | flops 384 | bytes 1536 | tf_op jit(solution)/shard_map/psum | solution.py:178
  631.8 51.6 %all-reduce.13.cloned.1.call-done = (bf16[3,768,192]{1,2,0:T(8,128)(2,1)}, bf16[192,768]{1,0:T(8,128)(2,1)}) async-done(((bf16[3,768,192]{1,2,0:T(8,128)(2,1)}, bf16[192,768]{1,0:T(8,128)(2,1)}), (bf16[3,768,192]{1,2,0:T(8,128)(2,1)}, bf16[192,768]{1,0:T(8,128)(2,1)})) %all-reduce.13.cloned.1.call-update) | async-done | bytes 1179664 | tf_op jit(solution)/shard_map/psum | solution.py:177
  685.2 2.5 convert_element_type.154
  687.7 45.4 %reduce-scatter.5.cloned.1.call-done = bf16[2,384,768]{2,1,0:T(8,128)(2,1)} async-done(((bf16[2,1536,768]{2,1,0:T(8,128)(2,1)}), bf16[2,384,768]{2,1,0:T(8,128)(2,1)}) %reduce-scatter.5.cloned.1.call-update) | async-done | bytes 1179664 | tf_op jit(solution)/shard_map/reduce_scatter | solution.py:171
  735.4 2.7 fusion.163
  738.3 3.0 convert_reduce_fusion.3
  741.2 12.3 all-reduce.2
  753.6 41.6 %all-reduce = (f32[768]{0:T(1024)}, f32[768]{0:T(1024)}, f32[768]{0:T(1024)}, f32[768]{0:T(1024)}, f32[768]{0:T(1024)}, /*index=5*/f32[3072]{0:T(1024)}, f32[768]{0:T(1024)}) all-reduce(f32[768]{0:T(1024)S(1)} %get-tuple-element.118, f32[768]{0:T(1024)S(1)} %get-tuple-element.119, ...), channel_id=1, replica_groups=mesh['dp'=8,'th'=2,'tw'=2] {'dp'}, use_global_device_ids=true, to_apply=%region_25.26 | all-reduce | flops 7680 | bytes 61440 | tf_op jit(solution)/shard_map/psum | solution.py:193
  795.2 512.1 %all-reduce.9.cloned.1.call-done = (f32[768,3072]{1,0:T(8,128)}, f32[3072,768]{1,0:T(8,128)}) async-done(((f32[768,3072]{1,0:T(8,128)}, f32[3072,768]{1,0:T(8,128)}), (f32[768,3072]{1,0:T(8,128)}, f32[3072,768]{1,0:T(8,128)})) %all-reduce.9.cloned.1.call-update) | async-done | bytes 18874384 | tf_op jit(solution)/shard_map/psum | solution.py:193
  1307.4 8.8 copy.61
  1316.2 3.7 copy.62
  (214 shorter events, 71.3 us)
Async XLA Ops:
  7.2 47.7 %copy-start = (bf16[3,768,192]{1,2,0:T(8,128)(2,1)S(1)}, bf16[3,768,192]{1,2,0:T(8,128)(2,1)}, u32[]{:S(2)}) copy-start(bf16[3,768,192]{1,2,0:T(8,128)(2,1)} %param.23) | copy-start | bytes 2654212
  7.2 7.5 copy-start.47
  7.2 47.7 %all-gather.3.cloned.1.call-start = ((), (), s32[]{:S(2)}) async-start(), calls=%async_computation.2 | async-start | bytes 5898240 | tf_op jit(solution)/shard_map/all_gather | solution.py:119
  8.8 2.3 copy-start.31
  14.6 159.1 %reduce-scatter.3.cloned.1.call-start = ((), (), s32[]{:S(2)}) async-start(), calls=%async_computation.3 | async-start | bytes 5898240 | tf_op jit(solution)/shard_map/reduce_scatter | solution.py:126
  14.8 46.8 %copy-start.20 = (s32[2,1536]{1,0:T(2,128)S(1)}, s32[2,1536]{1,0:T(2,128)}, u32[]{:S(2)}) copy-start(s32[2,1536]{1,0:T(2,128)} %param.20) | copy-start | bytes 36868
  120.7 5.0 copy-start.17
  120.7 53.0 %copy-start.5 = (bf16[2,384,768]{2,1,0:T(8,128)(2,1)S(1)}, bf16[2,384,768]{2,1,0:T(8,128)(2,1)}, u32[]{:S(2)}) copy-start(bf16[2,384,768]{2,1,0:T(8,128)(2,1)} %param.19) | copy-start | bytes 3538948
  120.7 53.0 %copy-start.21 = (f32[768]{0:T(1024)S(1)}, f32[768]{0:T(1024)}, u32[]{:S(2)}) copy-start(f32[768]{0:T(1024)} %param.26) | copy-start | bytes 9220
  125.7 51.8 %copy-start.25 = (f32[768]{0:T(1024)S(1)}, f32[768]{0:T(1024)}, u32[]{:S(2)}) copy-start(f32[768]{0:T(1024)} %param.27) | copy-start | bytes 9220
  125.7 51.8 %copy-start.30 = (f32[768]{0:T(1024)S(1)}, f32[768]{0:T(1024)}, u32[]{:S(2)}) copy-start(f32[768]{0:T(1024)} %param.28) | copy-start | bytes 9220
  125.7 51.8 %copy-start.44 = (f32[3072]{0:T(1024)S(1)}, f32[3072]{0:T(1024)}, u32[]{:S(2)}) copy-start(f32[3072]{0:T(1024)} %param.30) | copy-start | bytes 36868
  125.7 147.4 %all-gather.5.cloned.1.call-start = ((), (), s32[]{:S(2)}) async-start(), calls=%async_computation.4 | async-start | bytes 5898240 | tf_op jit(solution)/shard_map/all_gather | solution.py:160
  173.7 3.8 copy-start.7
  175.5 71.2 %copy-start.23 = (f32[2,384]{1,0:T(2,128)}, f32[2,384]{1,0:T(2,128)S(1)}, u32[]{:S(2)}) copy-start(f32[2,384]{1,0:T(2,128)S(1)} %broadcast_multiply_fusion) | copy-start | bytes 9220
  177.5 69.2 %copy-start.27 = (f32[2,384]{1,0:T(2,128)}, f32[2,384]{1,0:T(2,128)S(1)}, u32[]{:S(2)}) copy-start(f32[2,384]{1,0:T(2,128)S(1)} %fusion.183) | copy-start | bytes 9220
  186.7 23.4 %copy-start.15 = (bf16[2,384,768]{2,1,0:T(8,128)(2,1)S(1)}, bf16[2,384,768]{2,1,0:T(8,128)(2,1)}, u32[]{:S(2)}) copy-start(bf16[2,384,768]{2,1,0:T(8,128)(2,1)} %param.33) | copy-start | bytes 3538948
  230.7 4.7 copy-start.9
  230.7 4.7 copy-start.34
  232.7 14.0 %copy-start.38 = (f32[2,384]{1,0:T(2,128)}, f32[2,384]{1,0:T(2,128)S(1)}, u32[]{:S(2)}) copy-start(f32[2,384]{1,0:T(2,128)S(1)} %negate_multiply_fusion.2) | copy-start | bytes 9220
  235.4 363.2 %all-reduce.11.cloned.1.call-start = ((), (), s32[]{:S(2)}) async-start(), calls=%async_computation.7 | async-start | bytes 37748736 | tf_op jit(solution)/shard_map/psum | solution.py:193
  255.7 17.3 %copy-start.29 = (bf16[192,768]{1,0:T(8,128)(2,1)S(1)}, bf16[192,768]{1,0:T(8,128)(2,1)}, u32[]{:S(2)}) copy-start(bf16[192,768]{1,0:T(8,128)(2,1)} %param.25) | copy-start | bytes 884740
  255.8 427.6 %all-reduce.13.cloned.1.call-start = ((), (), s32[]{:S(2)}) async-start(), calls=%async_computation.8 | async-start | bytes 2359296 | tf_op jit(solution)/shard_map/psum | solution.py:177
  278.3 2.8 copy-start.1
  281.3 4.9 copy-start.12
  285.2 3.7 copy-start.2
  291.4 7.6 copy-start.4
  293.8 4.2 copy-start.3
  391.5 14.2 %copy-start.13 = (bf16[3,64,512]{2,1,0:T(8,128)(2,1)S(1)}, bf16[3,64,512]{2,1,0:T(8,128)(2,1)}, u32[]{:S(2)}) copy-start(bf16[3,64,512]{2,1,0:T(8,128)(2,1)} %fusion.377) | copy-start | bytes 589828 | tf_op jit(solution)/shard_map/while
  391.5 14.2 %copy-start.14 = (bf16[3,64,512]{2,1,0:T(8,128)(2,1)S(1)}, bf16[3,64,512]{2,1,0:T(8,128)(2,1)}, u32[]{:S(2)}) copy-start(bf16[3,64,512]{2,1,0:T(8,128)(2,1)} %fusion.378) | copy-start | bytes 589828 | tf_op jit(solution)/shard_map/while
  407.1 2.9 copy-start.1
  410.2 4.9 copy-start.12
  414.1 3.7 copy-start.2
  420.3 7.7 copy-start.4
  422.7 4.3 copy-start.3
  520.4 14.3 %copy-start.13 = (bf16[3,64,512]{2,1,0:T(8,128)(2,1)S(1)}, bf16[3,64,512]{2,1,0:T(8,128)(2,1)}, u32[]{:S(2)}) copy-start(bf16[3,64,512]{2,1,0:T(8,128)(2,1)} %fusion.377) | copy-start | bytes 589828 | tf_op jit(solution)/shard_map/while
  520.4 14.3 %copy-start.14 = (bf16[3,64,512]{2,1,0:T(8,128)(2,1)S(1)}, bf16[3,64,512]{2,1,0:T(8,128)(2,1)}, u32[]{:S(2)}) copy-start(bf16[3,64,512]{2,1,0:T(8,128)(2,1)} %fusion.378) | copy-start | bytes 589828 | tf_op jit(solution)/shard_map/while
  545.3 4.7 copy-start.18
  556.3 176.8 %reduce-scatter.5.cloned.1.call-start = ((), (), s32[]{:S(2)}) async-start(), calls=%async_computation.5 | async-start | bytes 5898240 | tf_op jit(solution)/shard_map/reduce_scatter | solution.py:171
  564.0 743.3 %all-reduce.9.cloned.1.call-start = ((), (), s32[]{:S(2)}) async-start(), calls=%async_computation.6 | async-start | bytes 37748736 | tf_op jit(solution)/shard_map/psum | solution.py:193
  598.7 1.3 copy-start.6
  598.7 1.6 copy-start.8
  598.7 1.6 copy-start.22
  598.7 1.6 copy-start.48
  600.3 8.8 copy-start.19
  609.1 124.0 %copy-start.32 = (f32[2,384]{1,0:T(2,128)S(1)}, f32[2,384]{1,0:T(2,128)}, u32[]{:S(2)}) copy-start(f32[2,384]{1,0:T(2,128)} %copy-done.31) | copy-start | bytes 9220
  609.1 124.0 %copy-start.33 = (f32[768]{0:T(1024)S(1)}, f32[768]{0:T(1024)}, u32[]{:S(2)}) copy-start(f32[768]{0:T(1024)} %param.21) | copy-start | bytes 9220
  609.1 126.3 %copy-start.41 = (f32[2,384]{1,0:T(2,128)S(1)}, f32[2,384]{1,0:T(2,128)}, u32[]{:S(2)}) copy-start(f32[2,384]{1,0:T(2,128)} %copy-done.40) | copy-start | bytes 9220
  609.1 126.3 %copy-start.37 = (f32[2,384]{1,0:T(2,128)S(1)}, f32[2,384]{1,0:T(2,128)}, u32[]{:S(2)}) copy-start(f32[2,384]{1,0:T(2,128)} %copy-done.36) | copy-start | bytes 9220
  609.5 128.7 %copy-start.24 = (f32[2,384]{1,0:T(2,128)S(1)}, f32[2,384]{1,0:T(2,128)}, u32[]{:S(2)}) copy-start(f32[2,384]{1,0:T(2,128)} %copy-done.23) | copy-start | bytes 9220
  609.5 128.7 %copy-start.26 = (f32[768]{0:T(1024)S(1)}, f32[768]{0:T(1024)}, u32[]{:S(2)}) copy-start(f32[768]{0:T(1024)} %param.27) | copy-start | bytes 9220
  609.5 128.7 %copy-start.28 = (f32[2,384]{1,0:T(2,128)S(1)}, f32[2,384]{1,0:T(2,128)}, u32[]{:S(2)}) copy-start(f32[2,384]{1,0:T(2,128)} %copy-done.27) | copy-start | bytes 9220
  609.5 128.7 %copy-start.35 = (f32[2,384]{1,0:T(2,128)S(1)}, f32[2,384]{1,0:T(2,128)}, u32[]{:S(2)}) copy-start(f32[2,384]{1,0:T(2,128)} %copy-done.34) | copy-start | bytes 9220
  609.5 128.7 %copy-start.39 = (f32[2,384]{1,0:T(2,128)S(1)}, f32[2,384]{1,0:T(2,128)}, u32[]{:S(2)}) copy-start(f32[2,384]{1,0:T(2,128)} %copy-done.38) | copy-start | bytes 9220
  733.1 5.1 copy-start.10
  733.1 5.1 copy-start.11
  733.1 5.1 copy-start.16
  738.1 3.1 copy-start.42
  738.1 3.1 copy-start.43
  738.1 3.1 copy-start.45
  738.1 3.1 copy-start.46
  1307.4 8.8 slice-start
  1307.4 8.8 slice-start.1
  1307.4 8.8 slice-start.2
  (2 other events, 1.2 us)
Sparse Core Ops, SparseCore 0:
  14.7 40.1 all-gather.2
  125.8 47.8 reduce-scatter.2
  235.6 37.4 all-gather.4
  276.3 322.3 all-reduce.10
  602.6 80.7 all-reduce.12
  685.9 47.1 reduce-scatter.4
  737.4 569.9 all-reduce.8
